TPU v7x, 32 devices: a whole 2x2x4 slice. The times are simulated.
32 devices in a mesh: layer: 8 (over y, x, core), tile: 4 (over z).
Axes of the slice: x: 2, y: 2, z: 4, core: 2. Of those that a mesh axis runs over, the one named last changes fastest.
Arguments:
- incident: bfloat16 [4096, 128], P('tile'), may hold values from -6 to 6
- interface: bfloat16 [16, 4096, 4096], P('layer', 'tile'), may hold values from -0.09375 to 0.09375
- eigvec: bfloat16 [16, 4096, 4096], P('layer', 'tile'), may hold values from -0.09375 to 0.09375
- angle: float32 [16, 4096], P('layer'), may hold values from -3.140625 to 3.140625
- decay: float32 [16, 4096], P('layer'), may hold values from 0.002 to 0.15
Outputs:
- fields: bfloat16 [16, 4096, 512], P('layer', 'tile')
- leaving: float32 [16, 4096, 128], P('layer', 'tile')
All inputs are finite; a program needn't handle non-finite values.
Results may differ from a plain program's by a relative error of at most 0.035.
Values sent between devices are 32-bit elements; how exact they have to be, the bound alone decides.
A program may use at most 128 MiB of HBM per device.

v0:
```python
import jax
import jax.numpy as jnp
from jax import lax
from jax.sharding import PartitionSpec as P

DEPTHS = 4


def shifted(x, axis, by):
    peers = lax.axis_size(axis)
    pairs = [(i, i + by) for i in range(peers) if 0 <= i + by < peers]
    return lax.ppermute(x, axis, pairs)


def rotate(block, angle_row, decay_row, frac):
    half = block.shape[1] // 2
    real_part = block[:, :half]
    imag_part = block[:, half:]
    scale = jnp.exp(-frac * decay_row)
    cosine = (scale * jnp.cos(frac * angle_row))[:, None]
    sine = (scale * jnp.sin(frac * angle_row))[:, None]
    return jnp.concatenate(
        [cosine * real_part - sine * imag_part, sine * real_part + cosine * imag_part], axis=1
    )


def advance(current, interface, angle, decay):
    fulls = []
    leaves = []
    for layer_num in range(interface.shape[0]):
        full = lax.all_gather(current, "tile", axis=0, tiled=True)
        fulls.append(full)
        phased = rotate(full, angle[layer_num], decay[layer_num], 1.0).astype(jnp.bfloat16)
        current = jnp.dot(interface[layer_num], phased, preferred_element_type=jnp.float32)
        leaves.append(current)
    return (jnp.stack(fulls), jnp.stack(leaves))


def pick_block(values, block_num, block_width, half):
    real_part = lax.dynamic_slice_in_dim(
        values, block_num * block_width, block_width, values.ndim - 1
    )
    imag_part = lax.dynamic_slice_in_dim(
        values, half + block_num * block_width, block_width, values.ndim - 1
    )
    return jnp.concatenate([real_part, imag_part], axis=values.ndim - 1)


def put_block(values, piece, block_num, block_width, half):
    last = values.ndim - 1
    real_piece = lax.slice_in_dim(piece, 0, block_width, axis=last)
    imag_piece = lax.slice_in_dim(piece, block_width, 2 * block_width, axis=last)
    values = lax.dynamic_update_slice_in_dim(values, real_piece, block_num * block_width, last)
    return lax.dynamic_update_slice_in_dim(values, imag_piece, half + block_num * block_width, last)


def on_device(incident, interface, eigvec, angle, decay):
    groups = lax.axis_size("layer")
    member = lax.axis_index("layer")
    layers_here = interface.shape[0]
    shard_rows = interface.shape[1]
    orders = interface.shape[2]
    width = incident.shape[1]
    half = width // 2
    start_amps = incident.astype(jnp.float32)
    store_full = jnp.zeros((layers_here, orders, width), jnp.float32)
    store_leave = jnp.zeros((layers_here, shard_rows, width), jnp.float32)
    block_count = 4
    block_width = half // block_count
    inbox = jnp.zeros((shard_rows, 2 * block_width), jnp.float32)

    def step_blocks(step, carry):
        inbox, store_full, store_leave = carry
        block_num = step - member
        valid = (block_num >= 0) & (block_num < block_count)
        clipped = jnp.clip(block_num, 0, block_count - 1)
        source = jnp.where(member == 0, pick_block(start_amps, clipped, block_width, half), inbox)
        fulls, leaves = advance(source, interface, angle, decay)
        store_full = jnp.where(
            valid, put_block(store_full, fulls, clipped, block_width, half), store_full
        )
        store_leave = jnp.where(
            valid, put_block(store_leave, leaves, clipped, block_width, half), store_leave
        )
        inbox = shifted(leaves[layers_here - 1], "layer", 1)
        return (inbox, store_full, store_leave)

    inbox, store_full, store_leave = lax.fori_loop(
        0, groups + block_count - 1, step_blocks, (inbox, store_full, store_leave)
    )
    fields = []
    for layer_num in range(layers_here):
        depth = jnp.concatenate(
            [
                rotate(
                    store_full[layer_num], angle[layer_num], decay[layer_num], step / DEPTHS
                ).astype(jnp.bfloat16)
                for step in range(DEPTHS)
            ],
            axis=1,
        )
        fields.append(
            jnp.dot(eigvec[layer_num], depth, preferred_element_type=jnp.float32).astype(
                jnp.bfloat16
            )
        )
    return (jnp.stack(fields), store_leave)


def solution(mesh):
    in_specs = (
        P("tile", None),
        P("layer", "tile", None),
        P("layer", "tile", None),
        P("layer", None),
        P("layer", None),
    )
    out_specs = (P("layer", "tile", None), P("layer", "tile", None))
    return jax.shard_map(
        on_device, mesh=mesh, in_specs=in_specs, out_specs=out_specs, check_vma=False
    )
```

profile of v0, /device:TPU:1, one launch (start us, length us, event | category | flops | bytes accessed | tf_op | source)
XLA Modules:
  0.0 704.2 jit_solution(1159093125117101727)
XLA Ops:
  11.3 665.6 %while.20 = (s32[]{:T(128)}, f32[1024,32]{0,1:T(8,128)S(1)}, f32[2,4096,128]{1,2,0:T(8,128)}, f32[2,1024,128]{1,2,0:T(8,128)S(1)}, f32[2,4096]{1,0:T(2,128)}, /*...) while((s32[]{:T(128)}, f32[1024,32]{0,1:T(8,128)S(1)}, ...), condition=%wide.region_1.2_spmd.clone, body=%wide.region_0.1_spmd.clone.sunk | while | flops 543318016 | bytes 56263120 | solution.py:88
  12.3 15.3 %all_gather.24 = f32[4096,32]{0,1:T(8,128)S(1)} all-gather(f32[1024,32]{0,1:T(8,128)S(1)} %maximum_select_fusion.2), channel_id=1, replica_groups=mesh['layer'=8,'tile'=4] {'tile'}, dimensions={0}, use_global_device_ids=true | all-gather | bytes 655360 | tf_op jit(solution)/shard_map/while/body/eval_jaxpr/all_gather | solution.py:31
  28.4 6.0 fusion.75
  34.4 11.9 %all_gather.25 = f32[4096,32]{0,1:T(8,128)S(1)} all-gather(f32[1024,32]{0,1:T(8,128)S(1)} %bitcast.104), channel_id=1, replica_groups=mesh['layer'=8,'tile'=4] {'tile'}, dimensions={0}, use_global_device_ids=true | all-gather | bytes 655360 | tf_op jit(solution)/shard_map/while/body/eval_jaxpr/all_gather | solution.py:31
  47.1 6.0 fusion.77
  53.0 9.5 %collective-permute-start = (f32[1024,32]{0,1:T(8,128)S(1)}, f32[1024,32]{0,1:T(8,128)S(1)}, u32[]{:S(2)}, u32[]{:S(2)}) collective-permute-start(f32[1024,32]{0,1:T(8,128)S(1)} %bitcast.107), channel_id=1, source_target_pairs={{0,4},{4,8},{8,12},{12,16},{16,20},{20,24},{24,28},{1,5},{5,9},{9,... | collective-permute-start | bytes 393224 | tf_op jit(solution)/shard_map/while/body/eval_jaxpr/ppermute | solution.py:12
  71.0 13.6 %all_gather.24 = f32[4096,32]{0,1:T(8,128)S(1)} all-gather(f32[1024,32]{0,1:T(8,128)S(1)} %maximum_select_fusion.2), channel_id=1, replica_groups=mesh['layer'=8,'tile'=4] {'tile'}, dimensions={0}, use_global_device_ids=true | all-gather | bytes 655360 | tf_op jit(solution)/shard_map/while/body/eval_jaxpr/all_gather | solution.py:31
  85.3 6.0 fusion.75
  91.3 11.9 %all_gather.25 = f32[4096,32]{0,1:T(8,128)S(1)} all-gather(f32[1024,32]{0,1:T(8,128)S(1)} %bitcast.104), channel_id=1, replica_groups=mesh['layer'=8,'tile'=4] {'tile'}, dimensions={0}, use_global_device_ids=true | all-gather | bytes 655360 | tf_op jit(solution)/shard_map/while/body/eval_jaxpr/all_gather | solution.py:31
  104.0 6.0 fusion.77
  109.9 8.0 %collective-permute-start = (f32[1024,32]{0,1:T(8,128)S(1)}, f32[1024,32]{0,1:T(8,128)S(1)}, u32[]{:S(2)}, u32[]{:S(2)}) collective-permute-start(f32[1024,32]{0,1:T(8,128)S(1)} %bitcast.107), channel_id=1, source_target_pairs={{0,4},{4,8},{8,12},{12,16},{16,20},{20,24},{24,28},{1,5},{5,9},{9,... | collective-permute-start | bytes 393224 | tf_op jit(solution)/shard_map/while/body/eval_jaxpr/ppermute | solution.py:12
  124.4 6.3 broadcast_select_fusion.9
  132.1 14.9 %all_gather.24 = f32[4096,32]{0,1:T(8,128)S(1)} all-gather(f32[1024,32]{0,1:T(8,128)S(1)} %maximum_select_fusion.2), channel_id=1, replica_groups=mesh['layer'=8,'tile'=4] {'tile'}, dimensions={0}, use_global_device_ids=true | all-gather | bytes 655360 | tf_op jit(solution)/shard_map/while/body/eval_jaxpr/all_gather | solution.py:31
  153.7 14.3 %all_gather.25 = f32[4096,32]{0,1:T(8,128)S(1)} all-gather(f32[1024,32]{0,1:T(8,128)S(1)} %bitcast.104), channel_id=1, replica_groups=mesh['layer'=8,'tile'=4] {'tile'}, dimensions={0}, use_global_device_ids=true | all-gather | bytes 655360 | tf_op jit(solution)/shard_map/while/body/eval_jaxpr/all_gather | solution.py:31
  168.8 6.0 fusion.77
  185.5 6.3 broadcast_select_fusion.9
  193.1 15.5 %all_gather.24 = f32[4096,32]{0,1:T(8,128)S(1)} all-gather(f32[1024,32]{0,1:T(8,128)S(1)} %maximum_select_fusion.2), channel_id=1, replica_groups=mesh['layer'=8,'tile'=4] {'tile'}, dimensions={0}, use_global_device_ids=true | all-gather | bytes 655360 | tf_op jit(solution)/shard_map/while/body/eval_jaxpr/all_gather | solution.py:31
  215.4 13.9 %all_gather.25 = f32[4096,32]{0,1:T(8,128)S(1)} all-gather(f32[1024,32]{0,1:T(8,128)S(1)} %bitcast.104), channel_id=1, replica_groups=mesh['layer'=8,'tile'=4] {'tile'}, dimensions={0}, use_global_device_ids=true | all-gather | bytes 655360 | tf_op jit(solution)/shard_map/while/body/eval_jaxpr/all_gather | solution.py:31
  230.1 6.0 fusion.77
  247.6 6.3 broadcast_select_fusion.9
  255.2 14.3 %all_gather.24 = f32[4096,32]{0,1:T(8,128)S(1)} all-gather(f32[1024,32]{0,1:T(8,128)S(1)} %maximum_select_fusion.2), channel_id=1, replica_groups=mesh['layer'=8,'tile'=4] {'tile'}, dimensions={0}, use_global_device_ids=true | all-gather | bytes 655360 | tf_op jit(solution)/shard_map/while/body/eval_jaxpr/all_gather | solution.py:31
  276.2 13.6 %all_gather.25 = f32[4096,32]{0,1:T(8,128)S(1)} all-gather(f32[1024,32]{0,1:T(8,128)S(1)} %bitcast.104), channel_id=1, replica_groups=mesh['layer'=8,'tile'=4] {'tile'}, dimensions={0}, use_global_device_ids=true | all-gather | bytes 655360 | tf_op jit(solution)/shard_map/while/body/eval_jaxpr/all_gather | solution.py:31
  308.7 6.3 broadcast_select_fusion.9
  316.4 14.3 %all_gather.24 = f32[4096,32]{0,1:T(8,128)S(1)} all-gather(f32[1024,32]{0,1:T(8,128)S(1)} %maximum_select_fusion.2), channel_id=1, replica_groups=mesh['layer'=8,'tile'=4] {'tile'}, dimensions={0}, use_global_device_ids=true | all-gather | bytes 655360 | tf_op jit(solution)/shard_map/while/body/eval_jaxpr/all_gather | solution.py:31
  337.4 13.9 %all_gather.25 = f32[4096,32]{0,1:T(8,128)S(1)} all-gather(f32[1024,32]{0,1:T(8,128)S(1)} %bitcast.104), channel_id=1, replica_groups=mesh['layer'=8,'tile'=4] {'tile'}, dimensions={0}, use_global_device_ids=true | all-gather | bytes 655360 | tf_op jit(solution)/shard_map/while/body/eval_jaxpr/all_gather | solution.py:31
  352.1 6.0 fusion.77
  376.7 13.5 %all_gather.24 = f32[4096,32]{0,1:T(8,128)S(1)} all-gather(f32[1024,32]{0,1:T(8,128)S(1)} %maximum_select_fusion.2), channel_id=1, replica_groups=mesh['layer'=8,'tile'=4] {'tile'}, dimensions={0}, use_global_device_ids=true | all-gather | bytes 655360 | tf_op jit(solution)/shard_map/while/body/eval_jaxpr/all_gather | solution.py:31
  391.0 6.0 fusion.75
  397.0 13.6 %all_gather.25 = f32[4096,32]{0,1:T(8,128)S(1)} all-gather(f32[1024,32]{0,1:T(8,128)S(1)} %bitcast.104), channel_id=1, replica_groups=mesh['layer'=8,'tile'=4] {'tile'}, dimensions={0}, use_global_device_ids=true | all-gather | bytes 655360 | tf_op jit(solution)/shard_map/while/body/eval_jaxpr/all_gather | solution.py:31
  417.3 7.9 %collective-permute-start = (f32[1024,32]{0,1:T(8,128)S(1)}, f32[1024,32]{0,1:T(8,128)S(1)}, u32[]{:S(2)}, u32[]{:S(2)}) collective-permute-start(f32[1024,32]{0,1:T(8,128)S(1)} %bitcast.107), channel_id=1, source_target_pairs={{0,4},{4,8},{8,12},{12,16},{16,20},{20,24},{24,28},{1,5},{5,9},{9,... | collective-permute-start | bytes 393224 | tf_op jit(solution)/shard_map/while/body/eval_jaxpr/ppermute | solution.py:12
  438.2 12.0 %all_gather.24 = f32[4096,32]{0,1:T(8,128)S(1)} all-gather(f32[1024,32]{0,1:T(8,128)S(1)} %maximum_select_fusion.2), channel_id=1, replica_groups=mesh['layer'=8,'tile'=4] {'tile'}, dimensions={0}, use_global_device_ids=true | all-gather | bytes 655360 | tf_op jit(solution)/shard_map/while/body/eval_jaxpr/all_gather | solution.py:31
  450.9 6.0 fusion.75
  456.9 14.2 %all_gather.25 = f32[4096,32]{0,1:T(8,128)S(1)} all-gather(f32[1024,32]{0,1:T(8,128)S(1)} %bitcast.104), channel_id=1, replica_groups=mesh['layer'=8,'tile'=4] {'tile'}, dimensions={0}, use_global_device_ids=true | all-gather | bytes 655360 | tf_op jit(solution)/shard_map/while/body/eval_jaxpr/all_gather | solution.py:31
  472.0 6.0 fusion.77
  477.9 7.3 %collective-permute-start = (f32[1024,32]{0,1:T(8,128)S(1)}, f32[1024,32]{0,1:T(8,128)S(1)}, u32[]{:S(2)}, u32[]{:S(2)}) collective-permute-start(f32[1024,32]{0,1:T(8,128)S(1)} %bitcast.107), channel_id=1, source_target_pairs={{0,4},{4,8},{8,12},{12,16},{16,20},{20,24},{24,28},{1,5},{5,9},{9,... | collective-permute-start | bytes 393224 | tf_op jit(solution)/shard_map/while/body/eval_jaxpr/ppermute | solution.py:12
  498.2 12.1 %all_gather.24 = f32[4096,32]{0,1:T(8,128)S(1)} all-gather(f32[1024,32]{0,1:T(8,128)S(1)} %maximum_select_fusion.2), channel_id=1, replica_groups=mesh['layer'=8,'tile'=4] {'tile'}, dimensions={0}, use_global_device_ids=true | all-gather | bytes 655360 | tf_op jit(solution)/shard_map/while/body/eval_jaxpr/all_gather | solution.py:31
  517.0 14.0 %all_gather.25 = f32[4096,32]{0,1:T(8,128)S(1)} all-gather(f32[1024,32]{0,1:T(8,128)S(1)} %bitcast.104), channel_id=1, replica_groups=mesh['layer'=8,'tile'=4] {'tile'}, dimensions={0}, use_global_device_ids=true | all-gather | bytes 655360 | tf_op jit(solution)/shard_map/while/body/eval_jaxpr/all_gather | solution.py:31
  537.8 7.2 %collective-permute-start = (f32[1024,32]{0,1:T(8,128)S(1)}, f32[1024,32]{0,1:T(8,128)S(1)}, u32[]{:S(2)}, u32[]{:S(2)}) collective-permute-start(f32[1024,32]{0,1:T(8,128)S(1)} %bitcast.107), channel_id=1, source_target_pairs={{0,4},{4,8},{8,12},{12,16},{16,20},{20,24},{24,28},{1,5},{5,9},{9,... | collective-permute-start | bytes 393224 | tf_op jit(solution)/shard_map/while/body/eval_jaxpr/ppermute | solution.py:12
  558.0 12.3 %all_gather.24 = f32[4096,32]{0,1:T(8,128)S(1)} all-gather(f32[1024,32]{0,1:T(8,128)S(1)} %maximum_select_fusion.2), channel_id=1, replica_groups=mesh['layer'=8,'tile'=4] {'tile'}, dimensions={0}, use_global_device_ids=true | all-gather | bytes 655360 | tf_op jit(solution)/shard_map/while/body/eval_jaxpr/all_gather | solution.py:31
  577.1 13.9 %all_gather.25 = f32[4096,32]{0,1:T(8,128)S(1)} all-gather(f32[1024,32]{0,1:T(8,128)S(1)} %bitcast.104), channel_id=1, replica_groups=mesh['layer'=8,'tile'=4] {'tile'}, dimensions={0}, use_global_device_ids=true | all-gather | bytes 655360 | tf_op jit(solution)/shard_map/while/body/eval_jaxpr/all_gather | solution.py:31
  591.8 6.0 fusion.77
  597.8 7.2 %collective-permute-start = (f32[1024,32]{0,1:T(8,128)S(1)}, f32[1024,32]{0,1:T(8,128)S(1)}, u32[]{:S(2)}, u32[]{:S(2)}) collective-permute-start(f32[1024,32]{0,1:T(8,128)S(1)} %bitcast.107), channel_id=1, source_target_pairs={{0,4},{4,8},{8,12},{12,16},{16,20},{20,24},{24,28},{1,5},{5,9},{9,... | collective-permute-start | bytes 393224 | tf_op jit(solution)/shard_map/while/body/eval_jaxpr/ppermute | solution.py:12
  617.9 12.3 %all_gather.24 = f32[4096,32]{0,1:T(8,128)S(1)} all-gather(f32[1024,32]{0,1:T(8,128)S(1)} %maximum_select_fusion.2), channel_id=1, replica_groups=mesh['layer'=8,'tile'=4] {'tile'}, dimensions={0}, use_global_device_ids=true | all-gather | bytes 655360 | tf_op jit(solution)/shard_map/while/body/eval_jaxpr/all_gather | solution.py:31
  636.9 14.3 %all_gather.25 = f32[4096,32]{0,1:T(8,128)S(1)} all-gather(f32[1024,32]{0,1:T(8,128)S(1)} %bitcast.104), channel_id=1, replica_groups=mesh['layer'=8,'tile'=4] {'tile'}, dimensions={0}, use_global_device_ids=true | all-gather | bytes 655360 | tf_op jit(solution)/shard_map/while/body/eval_jaxpr/all_gather | solution.py:31
  652.0 6.0 fusion.77
  658.0 6.9 collective-permute-start
  685.7 7.3 %fusion.35 = bf16[1,1024,512]{1,2,0:T(8,128)(2,1)S(1)} fusion(bf16[4096,512]{0,1:T(8,128)(2,1)S(1)} %fusion.45, bf16[2,1024,4096]{2,1,0:T(8,128)(2,1)} %param.9), kind=kOutput, calls=%fused_computation.51 | convolution fusion | flops 4295491584 | bytes 13631488 | tf_op jit(solution)/shard_map/dot_general | solution.py:103
  694.4 7.1 %fusion.32 = bf16[1,1024,512]{1,2,0:T(8,128)(2,1)S(1)} fusion(bf16[4096,512]{0,1:T(8,128)(2,1)S(1)} %fusion.53, bf16[2,1024,4096]{2,1,0:T(8,128)(2,1)} %param.9), kind=kOutput, calls=%fused_computation.50 | convolution fusion | flops 4295491584 | bytes 13631488 | tf_op jit(solution)/shard_map/dot_general | solution.py:103
  (290 shorter events, 237.3 us)
Async XLA Ops:
  11.3 1.0 copy-start.1
  53.0 16.9 %collective-permute-start = (f32[1024,32]{0,1:T(8,128)S(1)}, f32[1024,32]{0,1:T(8,128)S(1)}, u32[]{:S(2)}, u32[]{:S(2)}) collective-permute-start(f32[1024,32]{0,1:T(8,128)S(1)} %bitcast.107), channel_id=1, source_target_pairs={{0,4},{4,8},{8,12},{12,16},{16,20},{20,24},{24,28},{1,5},{5,9},{9,... | collective-permute-start | bytes 393224 | tf_op jit(solution)/shard_map/while/body/eval_jaxpr/ppermute | solution.py:12
  66.8 3.1 copy-start.2
  69.9 1.0 copy-start.1
  109.9 21.1 %collective-permute-start = (f32[1024,32]{0,1:T(8,128)S(1)}, f32[1024,32]{0,1:T(8,128)S(1)}, u32[]{:S(2)}, u32[]{:S(2)}) collective-permute-start(f32[1024,32]{0,1:T(8,128)S(1)} %bitcast.107), channel_id=1, source_target_pairs={{0,4},{4,8},{8,12},{12,16},{16,20},{20,24},{24,28},{1,5},{5,9},{9,... | collective-permute-start | bytes 393224 | tf_op jit(solution)/shard_map/while/body/eval_jaxpr/ppermute | solution.py:12
  124.4 6.6 copy-start.2
  131.1 1.0 copy-start.1
  174.8 17.3 %collective-permute-start = (f32[1024,32]{0,1:T(8,128)S(1)}, f32[1024,32]{0,1:T(8,128)S(1)}, u32[]{:S(2)}, u32[]{:S(2)}) collective-permute-start(f32[1024,32]{0,1:T(8,128)S(1)} %bitcast.107), channel_id=1, source_target_pairs={{0,4},{4,8},{8,12},{12,16},{16,20},{20,24},{24,28},{1,5},{5,9},{9,... | collective-permute-start | bytes 393224 | tf_op jit(solution)/shard_map/while/body/eval_jaxpr/ppermute | solution.py:12
  185.5 6.6 copy-start.2
  192.1 1.0 copy-start.1
  236.1 18.1 %collective-permute-start = (f32[1024,32]{0,1:T(8,128)S(1)}, f32[1024,32]{0,1:T(8,128)S(1)}, u32[]{:S(2)}, u32[]{:S(2)}) collective-permute-start(f32[1024,32]{0,1:T(8,128)S(1)} %bitcast.107), channel_id=1, source_target_pairs={{0,4},{4,8},{8,12},{12,16},{16,20},{20,24},{24,28},{1,5},{5,9},{9,... | collective-permute-start | bytes 393224 | tf_op jit(solution)/shard_map/while/body/eval_jaxpr/ppermute | solution.py:12
  247.6 6.6 copy-start.2
  254.2 1.0 copy-start.1
  296.6 18.7 %collective-permute-start = (f32[1024,32]{0,1:T(8,128)S(1)}, f32[1024,32]{0,1:T(8,128)S(1)}, u32[]{:S(2)}, u32[]{:S(2)}) collective-permute-start(f32[1024,32]{0,1:T(8,128)S(1)} %bitcast.107), channel_id=1, source_target_pairs={{0,4},{4,8},{8,12},{12,16},{16,20},{20,24},{24,28},{1,5},{5,9},{9,... | collective-permute-start | bytes 393224 | tf_op jit(solution)/shard_map/while/body/eval_jaxpr/ppermute | solution.py:12
  308.7 6.6 copy-start.2
  315.4 1.0 copy-start.1
  358.0 17.6 %collective-permute-start = (f32[1024,32]{0,1:T(8,128)S(1)}, f32[1024,32]{0,1:T(8,128)S(1)}, u32[]{:S(2)}, u32[]{:S(2)}) collective-permute-start(f32[1024,32]{0,1:T(8,128)S(1)} %bitcast.107), channel_id=1, source_target_pairs={{0,4},{4,8},{8,12},{12,16},{16,20},{20,24},{24,28},{1,5},{5,9},{9,... | collective-permute-start | bytes 393224 | tf_op jit(solution)/shard_map/while/body/eval_jaxpr/ppermute | solution.py:12
  370.3 5.3 copy-start.2
  375.7 1.0 copy-start.1
  417.3 19.8 %collective-permute-start = (f32[1024,32]{0,1:T(8,128)S(1)}, f32[1024,32]{0,1:T(8,128)S(1)}, u32[]{:S(2)}, u32[]{:S(2)}) collective-permute-start(f32[1024,32]{0,1:T(8,128)S(1)} %bitcast.107), channel_id=1, source_target_pairs={{0,4},{4,8},{8,12},{12,16},{16,20},{20,24},{24,28},{1,5},{5,9},{9,... | collective-permute-start | bytes 393224 | tf_op jit(solution)/shard_map/while/body/eval_jaxpr/ppermute | solution.py:12
  431.8 5.3 copy-start.2
  437.1 1.0 copy-start.1
  477.9 19.2 %collective-permute-start = (f32[1024,32]{0,1:T(8,128)S(1)}, f32[1024,32]{0,1:T(8,128)S(1)}, u32[]{:S(2)}, u32[]{:S(2)}) collective-permute-start(f32[1024,32]{0,1:T(8,128)S(1)} %bitcast.107), channel_id=1, source_target_pairs={{0,4},{4,8},{8,12},{12,16},{16,20},{20,24},{24,28},{1,5},{5,9},{9,... | collective-permute-start | bytes 393224 | tf_op jit(solution)/shard_map/while/body/eval_jaxpr/ppermute | solution.py:12
  491.8 5.3 copy-start.2
  497.2 1.0 copy-start.1
  537.8 19.1 %collective-permute-start = (f32[1024,32]{0,1:T(8,128)S(1)}, f32[1024,32]{0,1:T(8,128)S(1)}, u32[]{:S(2)}, u32[]{:S(2)}) collective-permute-start(f32[1024,32]{0,1:T(8,128)S(1)} %bitcast.107), channel_id=1, source_target_pairs={{0,4},{4,8},{8,12},{12,16},{16,20},{20,24},{24,28},{1,5},{5,9},{9,... | collective-permute-start | bytes 393224 | tf_op jit(solution)/shard_map/while/body/eval_jaxpr/ppermute | solution.py:12
  551.6 5.3 copy-start.2
  557.0 1.0 copy-start.1
  597.8 19.1 %collective-permute-start = (f32[1024,32]{0,1:T(8,128)S(1)}, f32[1024,32]{0,1:T(8,128)S(1)}, u32[]{:S(2)}, u32[]{:S(2)}) collective-permute-start(f32[1024,32]{0,1:T(8,128)S(1)} %bitcast.107), channel_id=1, source_target_pairs={{0,4},{4,8},{8,12},{12,16},{16,20},{20,24},{24,28},{1,5},{5,9},{9,... | collective-permute-start | bytes 393224 | tf_op jit(solution)/shard_map/while/body/eval_jaxpr/ppermute | solution.py:12
  611.6 5.3 copy-start.2
  616.9 1.0 copy-start.1
  658.0 18.9 %collective-permute-start = (f32[1024,32]{0,1:T(8,128)S(1)}, f32[1024,32]{0,1:T(8,128)S(1)}, u32[]{:S(2)}, u32[]{:S(2)}) collective-permute-start(f32[1024,32]{0,1:T(8,128)S(1)} %bitcast.107), channel_id=1, source_target_pairs={{0,4},{4,8},{8,12},{12,16},{16,20},{20,24},{24,28},{1,5},{5,9},{9,... | collective-permute-start | bytes 393224 | tf_op jit(solution)/shard_map/while/body/eval_jaxpr/ppermute | solution.py:12
  671.5 5.3 copy-start.2
  676.9 5.3 copy-start.15
  676.9 5.3 copy-start.16
  676.9 5.3 copy-start.17
  676.9 5.3 copy-start.18
  682.2 2.2 copy-start
  682.2 2.4 copy-start.13
  682.2 2.4 copy-start.14
  684.2 0.8 copy-start.11
  684.2 0.8 copy-start.12
  684.7 0.7 copy-start.9
  684.7 0.7 copy-start.10
  685.7 7.5 %copy-start.4 = (f32[1,4096]{1,0:T(1,128)S(1)}, f32[1,4096]{1,0:T(1,128)}, u32[]{:S(2)}) copy-start(f32[1,4096]{1,0:T(1,128)} %get-tuple-element.339) | copy-start | bytes 49156
  685.7 7.5 %copy-start.8 = (f32[1,4096]{1,0:T(1,128)S(1)}, f32[1,4096]{1,0:T(1,128)}, u32[]{:S(2)}) copy-start(f32[1,4096]{1,0:T(1,128)} %get-tuple-element.344) | copy-start | bytes 49156
  693.0 0.7 copy-start.7
  693.4 0.7 copy-start.6
  (2 other events, 1.4 us)
where the time goes:
time: 709 us; the launch traced here: 704 us
  blocking collectives  300 us (42%)
  other arithmetic  173 us (24%)
  matrix products  145 us (20%)
  starting transfers between devices  74.1 us (10%)
  local copies, waits for them, and re-layouts  9.94 us (1%)
    all_gather x22, blocking collectives, advance(): full = lax.all_gather(current, 'tile', axis=0, tiled=True)  300 us
    dot_general x22, matrix products, advance(): jnp.dot(interface[layer_num], phased, preferred_element_type=jnp.float32)  131 us
    ppermute x11, starting transfers between devices, shifted(): return lax.ppermute(x, axis, pairs)  74.1 us
    select_n x11, other arithmetic, step_blocks(): jnp.where(valid, put_block(store_full, fulls, clipped, block_width, half)...  57.7 us
    while x22, other arithmetic  50.2 us
    mul x24, other arithmetic, rotate(): cosine = (scale * jnp.cos(frac * angle_row))[:, None]  25.5 us
    dot_general x2, matrix products, on_device(): jnp.dot(eigvec[layer_num], depth, preferred_element_type=jnp.float32)  14.4 us
  transfers between devices with their start and end apart: 11, of which 0 were waited for; matrix products, arithmetic and copies ran while one was open for 19% of the time, Pallas kernels for 0%

commit v1 on v0

--- a/solution.py
+++ b/solution.py
@@ -28,7 +28,14 @@
     fulls = []
     leaves = []
     for layer_num in range(interface.shape[0]):
-        full = lax.all_gather(current, "tile", axis=0, tiled=True)
+        ring = [current]
+        for hop in range(3):
+            ring.append(lax.ppermute(ring[-1], "tile", [(dev, (dev + 1) % 4) for dev in range(4)]))
+        full = jnp.roll(
+            jnp.concatenate(ring[::-1], axis=0),
+            (lax.axis_index("tile") + 1) * ring[0].shape[0],
+            axis=0,
+        )
         fulls.append(full)
         phased = rotate(full, angle[layer_num], decay[layer_num], 1.0).astype(jnp.bfloat16)
         current = jnp.dot(interface[layer_num], phased, preferred_element_type=jnp.float32)

time: 709 us -> 724 us (1.021)
  waiting for transfers between devices: 0.03 us -> 355 us
  blocking collectives: 300 us -> 0 us
  other arithmetic: 173 us -> 78.5 us
  starting transfers between devices: 74.1 us -> 107 us
  local copies, waits for them, and re-layouts: 9.94 us -> 26 us
    ppermute x0 -> x66, waiting for transfers between devices: none -> 354 us  [advance(): lax.ppermute(ring[-1], 'tile', [(dev, (dev + 1) % 4) for dev in range(4)])]
    all_gather x22 -> x0, blocking collectives: 300 us -> none  [advance(): full = lax.all_gather(current, 'tile', axis=0, tiled=True)]
    select_n x11, other arithmetic: 57.7 us -> 13.9 us  [step_blocks(): jnp.where(valid, put_block(store_full, fulls, clipped, block_width, half)...]
    ppermute x11, starting transfers between devices: 74.1 us -> 104 us  [shifted(): return lax.ppermute(x, axis, pairs)]
    while x22, other arithmetic: 50.2 us -> 28 us
    mul x24, other arithmetic: 25.5 us -> 8.21 us  [rotate(): cosine = (scale * jnp.cos(frac * angle_row))[:, None]]
    while x44 -> x132, local copies, waits for them, and re-layouts: 0.11 us -> 16.8 us
    dynamic_update_slice x22, other arithmetic: 9.93 us -> 0.86 us  [put_block(): lax.dynamic_update_slice_in_dim(values, imag_piece, half + block_num * bl...]
  transfers between devices with their start and end apart: 11 -> 77, of which waited for: 0 -> 77; matrix products, arithmetic and copies ran while one was open for 19% -> 8% of each run, Pallas kernels for 0% -> 0%
where the time goes in v1:
time: 724 us; the launch traced here: 718 us
  waiting for transfers between devices  355 us (49%)
  matrix products  149 us (21%)
  starting transfers between devices  107 us (15%)
  other arithmetic  78.5 us (11%)
  local copies, waits for them, and re-layouts  26 us (4%)
    ppermute x66, waiting for transfers between devices, advance(): lax.ppermute(ring[-1], 'tile', [(dev, (dev + 1) % 4) for dev in range(4)])  354 us
    dot_general x22, matrix products, advance(): jnp.dot(interface[layer_num], phased, preferred_element_type=jnp.float32)  134 us
    ppermute x11, starting transfers between devices, shifted(): return lax.ppermute(x, axis, pairs)  104 us
    while x22, other arithmetic  28 us
    while x132, local copies, waits for them, and re-layouts  16.8 us
  transfers between devices with their start and end apart: 77, of which 77 were waited for; matrix products, arithmetic and copies ran while one was open for 8% of the time, Pallas kernels for 0%

profile of v1, /device:TPU:1, one launch (start us, length us, event | category | flops | bytes accessed | tf_op | source)
XLA Modules:
  0.0 718.2 jit_solution(16173596345799544350)
XLA Ops:
  9.9 681.7 %while.20 = (s32[]{:T(128)}, f32[1024,32]{0,1:T(8,128)S(1)}, f32[2,4096,128]{1,2,0:T(8,128)}, f32[2,1024,128]{1,2,0:T(8,128)S(1)}, f32[2,4096]{1,0:T(2,128)}, /*...) while((s32[]{:T(128)}, f32[1024,32]{0,1:T(8,128)S(1)}, ...), condition=%wide.region_1.3_spmd.clone, body=%wide.region_0.2_spmd.clone.sunk | while | flops 545153024 | bytes 127304736 | solution.py:95
  29.1 6.1 fusion.92
  46.4 6.6 collective-permute-done.5
  53.4 6.1 fusion.95
  59.5 10.2 %collective-permute-start.6 = (f32[1024,32]{0,1:T(8,128)S(1)}, f32[1024,32]{0,1:T(8,128)S(1)}, u32[]{:S(2)}, u32[]{:S(2)}) collective-permute-start(f32[1024,32]{0,1:T(8,128)S(1)} %bitcast.108), channel_id=1, source_target_pairs={{0,4},{4,8},{8,12},{12,16},{16,20},{20,24},{24,28},{1,5},{5,9},{9,... | collective-permute-start | bytes 393224 | tf_op jit(solution)/shard_map/while/body/eval_jaxpr/ppermute | solution.py:12
  85.6 6.5 collective-permute-done.2
  92.5 6.1 fusion.92
  115.9 6.1 fusion.95
  122.0 9.2 %collective-permute-start.6 = (f32[1024,32]{0,1:T(8,128)S(1)}, f32[1024,32]{0,1:T(8,128)S(1)}, u32[]{:S(2)}, u32[]{:S(2)}) collective-permute-start(f32[1024,32]{0,1:T(8,128)S(1)} %bitcast.108), channel_id=1, source_target_pairs={{0,4},{4,8},{8,12},{12,16},{16,20},{20,24},{24,28},{1,5},{5,9},{9,... | collective-permute-start | bytes 393224 | tf_op jit(solution)/shard_map/while/body/eval_jaxpr/ppermute | solution.py:12
  146.1 6.5 collective-permute-done.2
  153.0 6.1 fusion.92
  177.5 6.1 fusion.95
  183.6 9.7 %collective-permute-start.6 = (f32[1024,32]{0,1:T(8,128)S(1)}, f32[1024,32]{0,1:T(8,128)S(1)}, u32[]{:S(2)}, u32[]{:S(2)}) collective-permute-start(f32[1024,32]{0,1:T(8,128)S(1)} %bitcast.108), channel_id=1, source_target_pairs={{0,4},{4,8},{8,12},{12,16},{16,20},{20,24},{24,28},{1,5},{5,9},{9,... | collective-permute-start | bytes 393224 | tf_op jit(solution)/shard_map/while/body/eval_jaxpr/ppermute | solution.py:12
  214.0 6.1 fusion.92
  226.2 7.2 collective-permute-done.4
  233.4 6.4 collective-permute-done.5
  240.2 6.1 fusion.95
  246.3 8.7 %collective-permute-start.6 = (f32[1024,32]{0,1:T(8,128)S(1)}, f32[1024,32]{0,1:T(8,128)S(1)}, u32[]{:S(2)}, u32[]{:S(2)}) collective-permute-start(f32[1024,32]{0,1:T(8,128)S(1)} %bitcast.108), channel_id=1, source_target_pairs={{0,4},{4,8},{8,12},{12,16},{16,20},{20,24},{24,28},{1,5},{5,9},{9,... | collective-permute-start | bytes 393224 | tf_op jit(solution)/shard_map/while/body/eval_jaxpr/ppermute | solution.py:12
  258.5 6.1 collective-permute-done
  276.3 6.1 fusion.92
  293.8 7.0 collective-permute-done.5
  301.2 6.1 fusion.95
  307.3 9.4 %collective-permute-start.6 = (f32[1024,32]{0,1:T(8,128)S(1)}, f32[1024,32]{0,1:T(8,128)S(1)}, u32[]{:S(2)}, u32[]{:S(2)}) collective-permute-start(f32[1024,32]{0,1:T(8,128)S(1)} %bitcast.108), channel_id=1, source_target_pairs={{0,4},{4,8},{8,12},{12,16},{16,20},{20,24},{24,28},{1,5},{5,9},{9,... | collective-permute-start | bytes 393224 | tf_op jit(solution)/shard_map/while/body/eval_jaxpr/ppermute | solution.py:12
  320.3 7.1 collective-permute-done
  339.6 6.1 fusion.92
  363.0 6.1 fusion.95
  369.1 9.3 %collective-permute-start.6 = (f32[1024,32]{0,1:T(8,128)S(1)}, f32[1024,32]{0,1:T(8,128)S(1)}, u32[]{:S(2)}, u32[]{:S(2)}) collective-permute-start(f32[1024,32]{0,1:T(8,128)S(1)} %bitcast.108), channel_id=1, source_target_pairs={{0,4},{4,8},{8,12},{12,16},{16,20},{20,24},{24,28},{1,5},{5,9},{9,... | collective-permute-start | bytes 393224 | tf_op jit(solution)/shard_map/while/body/eval_jaxpr/ppermute | solution.py:12
  382.0 7.0 collective-permute-done
  401.1 6.1 fusion.92
  424.7 6.1 fusion.95
  430.8 9.4 %collective-permute-start.6 = (f32[1024,32]{0,1:T(8,128)S(1)}, f32[1024,32]{0,1:T(8,128)S(1)}, u32[]{:S(2)}, u32[]{:S(2)}) collective-permute-start(f32[1024,32]{0,1:T(8,128)S(1)} %bitcast.108), channel_id=1, source_target_pairs={{0,4},{4,8},{8,12},{12,16},{16,20},{20,24},{24,28},{1,5},{5,9},{9,... | collective-permute-start | bytes 393224 | tf_op jit(solution)/shard_map/while/body/eval_jaxpr/ppermute | solution.py:12
  443.8 7.1 collective-permute-done
  463.1 6.1 fusion.92
  486.6 6.1 fusion.95
  492.7 9.8 %collective-permute-start.6 = (f32[1024,32]{0,1:T(8,128)S(1)}, f32[1024,32]{0,1:T(8,128)S(1)}, u32[]{:S(2)}, u32[]{:S(2)}) collective-permute-start(f32[1024,32]{0,1:T(8,128)S(1)} %bitcast.108), channel_id=1, source_target_pairs={{0,4},{4,8},{8,12},{12,16},{16,20},{20,24},{24,28},{1,5},{5,9},{9,... | collective-permute-start | bytes 393224 | tf_op jit(solution)/shard_map/while/body/eval_jaxpr/ppermute | solution.py:12
  506.0 7.0 collective-permute-done
  525.5 6.1 fusion.92
  548.9 6.1 fusion.95
  555.0 9.2 %collective-permute-start.6 = (f32[1024,32]{0,1:T(8,128)S(1)}, f32[1024,32]{0,1:T(8,128)S(1)}, u32[]{:S(2)}, u32[]{:S(2)}) collective-permute-start(f32[1024,32]{0,1:T(8,128)S(1)} %bitcast.108), channel_id=1, source_target_pairs={{0,4},{4,8},{8,12},{12,16},{16,20},{20,24},{24,28},{1,5},{5,9},{9,... | collective-permute-start | bytes 393224 | tf_op jit(solution)/shard_map/while/body/eval_jaxpr/ppermute | solution.py:12
  567.8 6.9 collective-permute-done
  610.3 6.1 fusion.95
  616.4 9.8 %collective-permute-start.6 = (f32[1024,32]{0,1:T(8,128)S(1)}, f32[1024,32]{0,1:T(8,128)S(1)}, u32[]{:S(2)}, u32[]{:S(2)}) collective-permute-start(f32[1024,32]{0,1:T(8,128)S(1)} %bitcast.108), channel_id=1, source_target_pairs={{0,4},{4,8},{8,12},{12,16},{16,20},{20,24},{24,28},{1,5},{5,9},{9,... | collective-permute-start | bytes 393224 | tf_op jit(solution)/shard_map/while/body/eval_jaxpr/ppermute | solution.py:12
  629.8 7.1 collective-permute-done
  649.3 6.1 fusion.92
  672.7 6.1 fusion.95
  678.8 9.3 %collective-permute-start.6 = (f32[1024,32]{0,1:T(8,128)S(1)}, f32[1024,32]{0,1:T(8,128)S(1)}, u32[]{:S(2)}, u32[]{:S(2)}) collective-permute-start(f32[1024,32]{0,1:T(8,128)S(1)} %bitcast.108), channel_id=1, source_target_pairs={{0,4},{4,8},{8,12},{12,16},{16,20},{20,24},{24,28},{1,5},{5,9},{9,... | collective-permute-start | bytes 393224 | tf_op jit(solution)/shard_map/while/body/eval_jaxpr/ppermute | solution.py:12
  700.1 7.3 %fusion.49 = bf16[1,1024,512]{1,2,0:T(8,128)(2,1)S(1)} fusion(bf16[4096,512]{0,1:T(8,128)(2,1)S(1)} %fusion.59, bf16[2,1024,4096]{2,1,0:T(8,128)(2,1)} %param.11), kind=kOutput, calls=%fused_computation.81 | convolution fusion | flops 4295491584 | bytes 13631488 | tf_op jit(solution)/shard_map/dot_general | solution.py:110
  708.4 7.1 fusion.46
  (478 shorter events, 380.1 us)
Async XLA Ops:
  10.0 7.4 %collective-permute-start = (f32[1024,32]{0,1:T(8,128)S(1)}, f32[1024,32]{0,1:T(8,128)S(1)}, u32[]{:S(2)}, u32[]{:S(2)}) collective-permute-start(f32[1024,32]{0,1:T(8,128)S(1)} %maximum_select_fusion.2), channel_id=1, source_target_pairs={{0,1},{1,2},{2,3},{3,0},{4,5},{5,6},{6,7},{7,4},{8,9},{9,10},{10,1... | collective-permute-start | bytes 393224 | tf_op jit(solution)/shard_map/while/body/eval_jaxpr/ppermute | solution.py:33
  35.2 5.6 collective-permute-start.3
  46.4 6.6 collective-permute-start.5
  59.5 12.2 %collective-permute-start.6 = (f32[1024,32]{0,1:T(8,128)S(1)}, f32[1024,32]{0,1:T(8,128)S(1)}, u32[]{:S(2)}, u32[]{:S(2)}) collective-permute-start(f32[1024,32]{0,1:T(8,128)S(1)} %bitcast.108), channel_id=1, source_target_pairs={{0,4},{4,8},{8,12},{12,16},{16,20},{20,24},{24,28},{1,5},{5,9},{9,... | collective-permute-start | bytes 393224 | tf_op jit(solution)/shard_map/while/body/eval_jaxpr/ppermute | solution.py:12
  73.2 5.7 collective-permute-start
  78.9 6.7 collective-permute-start.1
  85.6 6.5 collective-permute-start.2
  98.6 5.6 collective-permute-start.3
  122.0 11.2 %collective-permute-start.6 = (f32[1024,32]{0,1:T(8,128)S(1)}, f32[1024,32]{0,1:T(8,128)S(1)}, u32[]{:S(2)}, u32[]{:S(2)}) collective-permute-start(f32[1024,32]{0,1:T(8,128)S(1)} %bitcast.108), channel_id=1, source_target_pairs={{0,4},{4,8},{8,12},{12,16},{16,20},{20,24},{24,28},{1,5},{5,9},{9,... | collective-permute-start | bytes 393224 | tf_op jit(solution)/shard_map/while/body/eval_jaxpr/ppermute | solution.py:12
  134.8 5.7 collective-permute-start
  146.1 6.5 collective-permute-start.2
  159.1 6.7 collective-permute-start.3
  183.6 11.6 %collective-permute-start.6 = (f32[1024,32]{0,1:T(8,128)S(1)}, f32[1024,32]{0,1:T(8,128)S(1)}, u32[]{:S(2)}, u32[]{:S(2)}) collective-permute-start(f32[1024,32]{0,1:T(8,128)S(1)} %bitcast.108), channel_id=1, source_target_pairs={{0,4},{4,8},{8,12},{12,16},{16,20},{20,24},{24,28},{1,5},{5,9},{9,... | collective-permute-start | bytes 393224 | tf_op jit(solution)/shard_map/while/body/eval_jaxpr/ppermute | solution.py:12
  196.7 5.7 collective-permute-start
  220.1 5.9 collective-permute-start.3
  226.1 7.3 %collective-permute-start.4 = (f32[1024,32]{0,1:T(8,128)S(1)}, f32[1024,32]{0,1:T(8,128)S(1)}, u32[]{:S(2)}, u32[]{:S(2)}) collective-permute-start(f32[1024,32]{0,1:T(8,128)S(1)} %collective-permute-done.3), channel_id=1, source_target_pairs={{0,1},{1,2},{2,3},{3,0},{4,5},{5,6},{6,7},{7,4},{8,9},{9,10},{10,1... | collective-permute-start | bytes 393224 | tf_op jit(solution)/shard_map/while/body/eval_jaxpr/ppermute | solution.py:33
  233.3 6.4 collective-permute-start.5
  246.3 10.6 %collective-permute-start.6 = (f32[1024,32]{0,1:T(8,128)S(1)}, f32[1024,32]{0,1:T(8,128)S(1)}, u32[]{:S(2)}, u32[]{:S(2)}) collective-permute-start(f32[1024,32]{0,1:T(8,128)S(1)} %bitcast.108), channel_id=1, source_target_pairs={{0,4},{4,8},{8,12},{12,16},{16,20},{20,24},{24,28},{1,5},{5,9},{9,... | collective-permute-start | bytes 393224 | tf_op jit(solution)/shard_map/while/body/eval_jaxpr/ppermute | solution.py:12
  258.5 6.2 collective-permute-start
  282.4 5.6 collective-permute-start.3
  288.1 5.7 collective-permute-start.4
  293.8 7.0 collective-permute-start.5
  307.3 11.4 %collective-permute-start.6 = (f32[1024,32]{0,1:T(8,128)S(1)}, f32[1024,32]{0,1:T(8,128)S(1)}, u32[]{:S(2)}, u32[]{:S(2)}) collective-permute-start(f32[1024,32]{0,1:T(8,128)S(1)} %bitcast.108), channel_id=1, source_target_pairs={{0,4},{4,8},{8,12},{12,16},{16,20},{20,24},{24,28},{1,5},{5,9},{9,... | collective-permute-start | bytes 393224 | tf_op jit(solution)/shard_map/while/body/eval_jaxpr/ppermute | solution.py:12
  320.2 7.1 collective-permute-start
  327.3 6.2 collective-permute-start.1
  345.7 5.6 collective-permute-start.3
  357.0 5.6 collective-permute-start.5
  369.1 11.3 %collective-permute-start.6 = (f32[1024,32]{0,1:T(8,128)S(1)}, f32[1024,32]{0,1:T(8,128)S(1)}, u32[]{:S(2)}, u32[]{:S(2)}) collective-permute-start(f32[1024,32]{0,1:T(8,128)S(1)} %bitcast.108), channel_id=1, source_target_pairs={{0,4},{4,8},{8,12},{12,16},{16,20},{20,24},{24,28},{1,5},{5,9},{9,... | collective-permute-start | bytes 393224 | tf_op jit(solution)/shard_map/while/body/eval_jaxpr/ppermute | solution.py:12
  381.9 7.0 collective-permute-start
  389.0 6.1 collective-permute-start.1
  407.2 5.6 collective-permute-start.3
  418.5 5.8 collective-permute-start.5
  430.8 11.4 %collective-permute-start.6 = (f32[1024,32]{0,1:T(8,128)S(1)}, f32[1024,32]{0,1:T(8,128)S(1)}, u32[]{:S(2)}, u32[]{:S(2)}) collective-permute-start(f32[1024,32]{0,1:T(8,128)S(1)} %bitcast.108), channel_id=1, source_target_pairs={{0,4},{4,8},{8,12},{12,16},{16,20},{20,24},{24,28},{1,5},{5,9},{9,... | collective-permute-start | bytes 393224 | tf_op jit(solution)/shard_map/while/body/eval_jaxpr/ppermute | solution.py:12
  443.7 7.1 collective-permute-start
  450.9 6.2 collective-permute-start.1
  469.2 5.6 collective-permute-start.3
  480.5 5.6 collective-permute-start.5
  492.7 11.8 %collective-permute-start.6 = (f32[1024,32]{0,1:T(8,128)S(1)}, f32[1024,32]{0,1:T(8,128)S(1)}, u32[]{:S(2)}, u32[]{:S(2)}) collective-permute-start(f32[1024,32]{0,1:T(8,128)S(1)} %bitcast.108), channel_id=1, source_target_pairs={{0,4},{4,8},{8,12},{12,16},{16,20},{20,24},{24,28},{1,5},{5,9},{9,... | collective-permute-start | bytes 393224 | tf_op jit(solution)/shard_map/while/body/eval_jaxpr/ppermute | solution.py:12
  506.0 7.0 collective-permute-start
  513.0 6.5 collective-permute-start.1
  555.0 11.2 %collective-permute-start.6 = (f32[1024,32]{0,1:T(8,128)S(1)}, f32[1024,32]{0,1:T(8,128)S(1)}, u32[]{:S(2)}, u32[]{:S(2)}) collective-permute-start(f32[1024,32]{0,1:T(8,128)S(1)} %bitcast.108), channel_id=1, source_target_pairs={{0,4},{4,8},{8,12},{12,16},{16,20},{20,24},{24,28},{1,5},{5,9},{9,... | collective-permute-start | bytes 393224 | tf_op jit(solution)/shard_map/while/body/eval_jaxpr/ppermute | solution.py:12
  567.7 6.9 collective-permute-start
  574.6 6.0 collective-permute-start.1
  604.1 5.9 collective-permute-start.5
  616.4 11.7 %collective-permute-start.6 = (f32[1024,32]{0,1:T(8,128)S(1)}, f32[1024,32]{0,1:T(8,128)S(1)}, u32[]{:S(2)}, u32[]{:S(2)}) collective-permute-start(f32[1024,32]{0,1:T(8,128)S(1)} %bitcast.108), channel_id=1, source_target_pairs={{0,4},{4,8},{8,12},{12,16},{16,20},{20,24},{24,28},{1,5},{5,9},{9,... | collective-permute-start | bytes 393224 | tf_op jit(solution)/shard_map/while/body/eval_jaxpr/ppermute | solution.py:12
  629.7 7.1 collective-permute-start
  636.8 6.5 collective-permute-start.1
  678.8 11.2 %collective-permute-start.6 = (f32[1024,32]{0,1:T(8,128)S(1)}, f32[1024,32]{0,1:T(8,128)S(1)}, u32[]{:S(2)}, u32[]{:S(2)}) collective-permute-start(f32[1024,32]{0,1:T(8,128)S(1)} %bitcast.108), channel_id=1, source_target_pairs={{0,4},{4,8},{8,12},{12,16},{16,20},{20,24},{24,28},{1,5},{5,9},{9,... | collective-permute-start | bytes 393224 | tf_op jit(solution)/shard_map/while/body/eval_jaxpr/ppermute | solution.py:12
  (96 other events, 775.8 us)
